TPU v7x, 256 devices: a whole 4x4x8 slice. The times are simulated.
256 devices in a mesh: row: 32 (over z, y_lo, core), col: 8 (over y_hi, x).
Axes of the slice: x: 4, y: 4 (y_hi: 2, y_lo: 2; y = y_hi * 2 + y_lo), z: 8, core: 2. Of those that a mesh axis runs over, the one named last changes fastest.
Arguments:
- coupling: bfloat16 [16384, 4096], P('row', 'col'), may hold values from 0.19921875 to 5
- source_dist: bfloat16 [16384, 16384], P('row'), may hold values from -0.013531647 to 0.013531647, as said below
- target_dist: bfloat16 [4096, 4096], P('row', 'col'), may hold values from -0.09375 to 0.09375
- source_feat: bfloat16 [16384, 256], P('row'), may hold values from -3.5 to 3.5
- target_feat: bfloat16 [4096, 256], P('col'), may hold values from -3.5 to 3.5
- source_type: int32 [16384], P('row'), may hold values from 0 to 15
- target_type: int32 [4096], P('col'), may hold values from 0 to 15
- row_weight: float32 [16384], P('row'), may hold values from 0.5 to 10
- col_weight: float32 [4096], P('col'), may hold values from 0.5 to 2
Outputs:
- coupling_next: bfloat16 [16384, 4096], P('row', 'col')
- barycentre: bfloat16 [16384, 256], P(('row', 'col'))
Inputs may be any that keep to these rules, and one draw needn't show every extreme that they name: `source_dist`: symmetric.
All inputs are finite; a program needn't handle non-finite values.
Results may differ from a plain program's by a relative error of at most 0.02.
Values may be sent and summed in bfloat16 or wider, within the bound.
A program may use at most 128 MiB of HBM per device.

v0:
```python
import math
import jax
import jax.numpy as jnp
from jax import lax
from jax.sharding import PartitionSpec as P

coupling_weight = 0.5
feature_weight = 2.5
mismatch_cost = 1.0


def from_everyone(value, axis):
    copies = jnp.broadcast_to(value, (lax.axis_size(axis), *value.shape))
    return lax.all_to_all(copies, axis, split_axis=0, concat_axis=0, tiled=True)


def all_in_one(value, axis):
    leaves = jax.tree.leaves(value)
    turns = sorted(range(len(leaves)), key=lambda k: -leaves[k].size)
    width = (1, *leaves[turns[0]].shape)[-1]
    lines = [
        jnp.pad(leaves[k].reshape(-1), (0, -leaves[k].size % width)).reshape(-1, width)
        for k in turns
    ]
    both, at, found = (from_everyone(jnp.concatenate(lines), axis), 0, {})
    for k, line in zip(turns, lines):
        share = both[:, at : at + len(line)].reshape(len(both), -1)
        found[k] = share[:, : leaves[k].size].reshape(-1, *leaves[k].shape)
        at += len(line)
    numbers = iter(range(len(leaves)))
    return jax.tree.map(lambda _: found[next(numbers)], value)


def combined_pairwise(pieces, combine):
    while len(jax.tree.leaves(pieces)[0]) > 1:
        pieces = jax.vmap(combine)(
            *(jax.tree.map(lambda part: part[side::2], pieces) for side in (0, 1))
        )
    return jax.tree.map(lambda part: part[0], pieces)


def combined_all(value, axis, combine):
    pieces = all_in_one(value, axis)
    return combined_pairwise(pieces, combine)


def gathered_by_type(value, axis):
    leaves, found = (jax.tree.leaves(value), {})
    for first, a in enumerate(leaves):
        if first not in found:
            alike = [k for k, b in enumerate(leaves) if b.dtype == a.dtype]
            got = (
                all_in_one([leaves[k] for k in alike], axis)
                if len(alike) > 1
                else [from_everyone(a, axis)]
            )
            for k, b in zip(alike, got):
                found[k] = b
    numbers = iter(range(len(leaves)))
    return jax.tree.map(lambda _: found[next(numbers)], value)


def combined_all_2(value, axis, combine):
    pieces = gathered_by_type(value, axis)
    return combined_pairwise(pieces, combine)


def split_up(value, dim, length):
    lengths = value.shape
    pieces = value.reshape(*lengths[:dim], length, lengths[dim] // length, *lengths[dim + 1 :])
    return jnp.moveaxis(pieces, dim, 0)


def summed_on_arrival(value, axis, dim):
    length = lax.axis_size(axis)
    pieces = lax.all_to_all(split_up(value, dim, length), axis, 0, 0, tiled=True)
    return jnp.sum(pieces.astype(jnp.float32), axis=0)


def combine_stats(earlier, later):
    highest = jnp.maximum(earlier[0], later[0])
    return (
        highest,
        earlier[1] * jnp.exp(earlier[0] - highest) + later[1] * jnp.exp(later[0] - highest),
    )


def shards(
    coupling,
    source_dist,
    target_dist,
    source_feat,
    target_feat,
    source_type,
    target_type,
    row_weight,
    col_weight,
):
    row_count, col_count = coupling.shape
    feat_width = source_feat.shape[1]
    total_rows = row_count * lax.axis_size("row")
    total_cols = col_count * lax.axis_size("col")
    target_block = lax.all_gather(target_dist, "row", axis=0, tiled=True)
    first = jnp.dot(
        source_dist,
        lax.all_gather(coupling, "row", axis=0, tiled=True),
        preferred_element_type=jnp.float32,
    )
    first_whole = lax.all_gather(first.astype(jnp.bfloat16), "col", axis=1, tiled=True)
    second = jnp.dot(first_whole, target_block, preferred_element_type=jnp.float32)
    affinity = lax.dot_general(
        source_feat, target_feat, (((1,), (1,)), ((), ())), preferred_element_type=jnp.float32
    )
    mismatch = (source_type[:, None] != target_type[None, :]).astype(jnp.float32)
    score = (
        jnp.log(coupling.astype(jnp.float32))
        + coupling_weight * second
        + feature_weight / math.sqrt(feat_width) * affinity
        - mismatch_cost * mismatch
    )
    local_top = jnp.max(score, axis=1)
    local_sum = jnp.sum(jnp.exp(score - local_top[:, None]), axis=1)
    row_top, row_sum = combined_all((local_top, local_sum), "col", combine_stats)
    row_lse = row_top + jnp.log(row_sum)
    first_log = score - row_lse[:, None] + jnp.log(row_weight)[:, None] + math.log(total_cols)
    local_col_top = jnp.max(first_log, axis=0)
    local_col_sum = jnp.sum(jnp.exp(first_log - local_col_top[None, :]), axis=0)
    col_top, col_sum = combined_all_2((local_col_top, local_col_sum), "row", combine_stats)
    col_lse = col_top + jnp.log(col_sum)
    next_float = jnp.exp(
        first_log - col_lse[None, :] + jnp.log(col_weight)[None, :] + math.log(total_rows)
    )
    coupling_next = next_float.astype(jnp.bfloat16)
    numer = jnp.dot(coupling_next, target_feat, preferred_element_type=jnp.float32)
    mass = jnp.sum(next_float, axis=1, keepdims=True)
    numer_home, mass_home = (
        summed_on_arrival(numer.astype(jnp.bfloat16), "col", 0),
        summed_on_arrival(mass.astype(jnp.bfloat16), "col", 0),
    )
    return (coupling_next, (numer_home / mass_home).astype(jnp.bfloat16))


def solution(mesh):
    in_specs = (
        P("row", "col"),
        P("row", None),
        P("row", "col"),
        P("row", None),
        P("col", None),
        P("row"),
        P("col"),
        P("row"),
        P("col"),
    )
    out_specs = (P("row", "col"), P(("row", "col"), None))
    return jax.shard_map(shards, mesh=mesh, in_specs=in_specs, out_specs=out_specs, check_vma=False)
```

profile of v0, /device:TPU:8, one launch (start us, length us, event | category | flops | bytes accessed | tf_op | source)
XLA Modules:
  0.0 336.4 jit_solution(761586258189664936)
XLA Ops:
  7.2 0.0 copy-start
  7.2 0.0 all-gather.4.cloned.1.call-start
  7.2 0.7 all-gather.4.cloned.1.call-update
  7.9 0.0 all-gather.8.cloned.1.call-start
  8.0 0.7 all-gather.8.cloned.1.call-update
  8.7 0.0 copy-start.1
  8.7 0.0 all-gather.6.cloned.1.call-start
  8.7 103.6 %all-gather.4.cloned.1.call-done = bf16[16384,512]{1,0:T(8,128)(2,1)} async-done(((bf16[512,512]{1,0:T(8,128)(2,1)}), bf16[16384,512]{1,0:T(8,128)(2,1)}) %all-gather.4.cloned.1.call-update) | async-done | bytes 16777232 | tf_op jit(solution)/shard_map/all_gather | solution.py:106
  112.4 17.9 %convolution_convert_fusion = bf16[512,512]{1,0:T(8,128)(2,1)} fusion(bf16[512,16384]{1,0:T(8,128)(2,1)} %param.10, bf16[16384,512]{1,0:T(8,128)(2,1)} %all-gather.4.cloned.1.call-done), kind=kOutput, calls=%fused_computation.5 | convolution fusion | flops 8590196736 | bytes 34078720 | tf_op jit(solution)/shard_map/dot_general | solution.py:104
  130.2 0.0 copy-start.2
  130.2 0.0 copy-start.5
  130.2 0.0 copy-start.6
  130.2 0.0 copy-start.3
  130.2 0.0 copy-start.4
  130.3 0.0 all-gather.6.cloned.1.call-update
  130.3 0.0 copy-done.1
  130.3 0.2 copy.19
  130.5 50.3 %all-gather.8.cloned.1.call-done = bf16[4096,512]{1,0:T(8,128)(2,1)} async-done(((bf16[128,512]{1,0:T(8,128)(2,1)}), bf16[4096,512]{1,0:T(8,128)(2,1)}) %all-gather.8.cloned.1.call-update) | async-done | bytes 4194320 | tf_op jit(solution)/shard_map/all_gather | solution.py:103
  180.8 84.8 %all-gather.6.cloned.1.call-done = bf16[512,4096]{1,0:T(8,128)(2,1)} async-done(((bf16[512,512]{1,0:T(8,128)(2,1)}), bf16[512,4096]{1,0:T(8,128)(2,1)}) %all-gather.6.cloned.1.call-update) | async-done | bytes 4194320 | tf_op jit(solution)/shard_map/all_gather | solution.py:109
  265.6 5.9 %fusion.2 = f32[512,512]{0,1:T(8,128)S(1)} fusion(bf16[512,4096]{1,0:T(8,128)(2,1)} %all-gather.6.cloned.1.call-done, bf16[4096,512]{1,0:T(8,128)(2,1)} %all-gather.8.cloned.1.call-done, bf16[512,512]{0,1:T(8,128)(2,1)S(1)} %copy.19), kind=kOutput, calls=%fused_computation.4 | convolution fusion | flops 2148270080 | bytes 9961472 | tf_op jit(solution)/shard_map/dot_general | solution.py:110
  271.5 0.0 copy-done
  271.5 0.0 copy-done.2
  271.5 0.0 copy-done.5
  271.5 0.0 copy-done.6
  271.5 0.4 fusion.12
  271.9 0.2 exponential_reduce_fusion.1
  272.1 0.6 broadcast_in_dim.4
  272.8 4.5 %all-to-all-start = ((f32[8,2,512]{2,1,0:T(2,128)}), f32[8,2,512]{2,1,0:T(2,128)S(1)}, u32[]{:S(2)}, u32[]{:S(2)}) async-start(f32[8,2,512]{2,1,0:T(2,128)} %broadcast_in_dim.4), calls=%async_computation | async-start | bytes 65536 | tf_op jit(solution)/shard_map/all_to_all | solution.py:14
  277.3 0.0 copy-done.3
  277.3 7.7 %all-to-all-done = f32[8,2,512]{2,1,0:T(2,128)S(1)} async-done(((f32[8,2,512]{2,1,0:T(2,128)}), f32[8,2,512]{2,1,0:T(2,128)S(1)}, u32[]{:S(2)}, u32[]{:S(2)}) %all-to-all-start) | async-done | bytes 32800 | tf_op jit(solution)/shard_map/all_to_all | solution.py:14
  285.3 0.2 fusion.5
  285.6 0.4 exponential_reduce_fusion
  285.9 0.7 broadcast_in_dim.5
  286.6 8.6 %all-to-all-start.1 = ((f32[32,2,512]{2,1,0:T(2,128)}), f32[32,2,512]{2,1,0:T(2,128)S(1)}, u32[]{:S(2)}, u32[]{:S(2)}) async-start(f32[32,2,512]{2,1,0:T(2,128)} %broadcast_in_dim.5), calls=%async_computation.1 | async-start | bytes 262144 | tf_op jit(solution)/shard_map/all_to_all | solution.py:14
  295.3 0.0 copy-done.4
  295.3 9.2 %all-to-all-done.1 = f32[32,2,512]{2,1,0:T(2,128)S(1)} async-done(((f32[32,2,512]{2,1,0:T(2,128)}), f32[32,2,512]{2,1,0:T(2,128)S(1)}, u32[]{:S(2)}, u32[]{:S(2)}) %all-to-all-start.1) | async-done | bytes 131104 | tf_op jit(solution)/shard_map/all_to_all | solution.py:14
  304.5 0.1 fusion.10
  305.1 0.4 fusion.3
  305.5 0.7 convert_element_type.49
  306.2 3.3 all-to-all-start.3
  309.5 1.1 convolution_convert_fusion.1
  310.5 6.5 %all-to-all-done.3 = bf16[8,64,1]{1,2,0:T(2,128)(2,1)S(1)} async-done(((bf16[8,64,1]{1,2,0:T(2,128)(2,1)}), bf16[8,64,1]{1,2,0:T(2,128)(2,1)S(1)}, u32[]{:S(2)}, u32[]{:S(2)}) %all-to-all-start.3) | async-done | bytes 1056 | tf_op jit(solution)/shard_map/all_to_all | solution.py:76
  317.0 3.4 %all-to-all-start.2 = ((bf16[8,64,256]{2,1,0:T(8,128)(2,1)}), bf16[8,64,256]{2,1,0:T(8,128)(2,1)S(1)}, u32[]{:S(2)}, u32[]{:S(2)}) async-start(bf16[8,64,256]{2,1,0:T(8,128)(2,1)} %bitcast.8), calls=%async_computation.2 | async-start | bytes 524288 | tf_op jit(solution)/shard_map/all_to_all | solution.py:76
  320.4 1.0 copy.23
  321.5 7.7 %all-to-all-done.2 = bf16[8,64,256]{2,1,0:T(8,128)(2,1)S(1)} async-done(((bf16[8,64,256]{2,1,0:T(8,128)(2,1)}), bf16[8,64,256]{2,1,0:T(8,128)(2,1)S(1)}, u32[]{:S(2)}, u32[]{:S(2)}) %all-to-all-start.2) | async-done | bytes 262176 | tf_op jit(solution)/shard_map/all_to_all | solution.py:76
  329.2 0.7 divide_convert_fusion
  (42 shorter events, 0.8 us)
Async XLA Ops:
  7.2 264.3 %copy-start = (bf16[512,256]{1,0:T(8,128)(2,1)S(1)}, bf16[512,256]{1,0:T(8,128)(2,1)}, u32[]{:S(2)}) copy-start(bf16[512,256]{1,0:T(8,128)(2,1)} %param.13) | copy-start | bytes 786436
  7.2 105.2 %all-gather.4.cloned.1.call-start = ((), (), s32[]{:S(2)}) async-start(), calls=%async_computation.4 | async-start | bytes 17301504 | tf_op jit(solution)/shard_map/all_gather | solution.py:106
  7.9 172.9 %all-gather.8.cloned.1.call-start = ((), (), s32[]{:S(2)}) async-start(), calls=%async_computation.6 | async-start | bytes 4325376 | tf_op jit(solution)/shard_map/all_gather | solution.py:103
  8.7 121.6 %copy-start.1 = (bf16[512,512]{1,0:T(8,128)(2,1)S(1)}, bf16[512,512]{1,0:T(8,128)(2,1)}, u32[]{:S(2)}) copy-start(bf16[512,512]{1,0:T(8,128)(2,1)} %param.9) | copy-start | bytes 1572868
  8.7 256.9 %all-gather.6.cloned.1.call-start = ((), (), s32[]{:S(2)}) async-start(), calls=%async_computation.5 | async-start | bytes 4718592 | tf_op jit(solution)/shard_map/all_gather | solution.py:109
  130.2 141.3 %copy-start.2 = (bf16[512,256]{1,0:T(8,128)(2,1)S(1)}, bf16[512,256]{1,0:T(8,128)(2,1)}, u32[]{:S(2)}) copy-start(bf16[512,256]{1,0:T(8,128)(2,1)} %param.12) | copy-start | bytes 786436
  130.2 141.3 %copy-start.5 = (s32[512]{0:T(512)S(1)}, s32[512]{0:T(512)}, u32[]{:S(2)}) copy-start(s32[512]{0:T(512)} %param.15) | copy-start | bytes 6148
  130.2 141.3 %copy-start.6 = (s32[512]{0:T(512)S(1)}, s32[512]{0:T(512)}, u32[]{:S(2)}) copy-start(s32[512]{0:T(512)} %param.14) | copy-start | bytes 6148
  130.2 147.0 %copy-start.3 = (f32[512]{0:T(512)S(1)}, f32[512]{0:T(512)}, u32[]{:S(2)}) copy-start(f32[512]{0:T(512)} %param.16) | copy-start | bytes 6148
  130.2 165.0 %copy-start.4 = (f32[512]{0:T(512)S(1)}, f32[512]{0:T(512)}, u32[]{:S(2)}) copy-start(f32[512]{0:T(512)} %param.17) | copy-start | bytes 6148
  272.8 12.3 %all-to-all-start = ((f32[8,2,512]{2,1,0:T(2,128)}), f32[8,2,512]{2,1,0:T(2,128)S(1)}, u32[]{:S(2)}, u32[]{:S(2)}) async-start(f32[8,2,512]{2,1,0:T(2,128)} %broadcast_in_dim.4), calls=%async_computation | async-start | bytes 65536 | tf_op jit(solution)/shard_map/all_to_all | solution.py:14
  286.6 17.9 %all-to-all-start.1 = ((f32[32,2,512]{2,1,0:T(2,128)}), f32[32,2,512]{2,1,0:T(2,128)S(1)}, u32[]{:S(2)}, u32[]{:S(2)}) async-start(f32[32,2,512]{2,1,0:T(2,128)} %broadcast_in_dim.5), calls=%async_computation.1 | async-start | bytes 262144 | tf_op jit(solution)/shard_map/all_to_all | solution.py:14
  306.2 10.9 %all-to-all-start.3 = ((bf16[8,64,1]{1,2,0:T(2,128)(2,1)}), bf16[8,64,1]{1,2,0:T(2,128)(2,1)S(1)}, u32[]{:S(2)}, u32[]{:S(2)}) async-start(bf16[8,64,1]{1,2,0:T(2,128)(2,1)} %convert_element_type.49), calls=%async_computation.3 | async-start | bytes 8192 | tf_op jit(solution)/shard_map/all_to_all | solution.py:76
  317.0 12.1 %all-to-all-start.2 = ((bf16[8,64,256]{2,1,0:T(8,128)(2,1)}), bf16[8,64,256]{2,1,0:T(8,128)(2,1)S(1)}, u32[]{:S(2)}, u32[]{:S(2)}) async-start(bf16[8,64,256]{2,1,0:T(8,128)(2,1)} %bitcast.8), calls=%async_computation.2 | async-start | bytes 524288 | tf_op jit(solution)/shard_map/all_to_all | solution.py:76
Sparse Core Ops, SparseCore 0:
  9.8 102.4 all-gather.3
  114.2 66.5 all-gather.7
  183.9 81.6 all-gather.5
where the time goes:
time: 337 us; the launch traced here: 336 us
  waiting for transfers between devices  271 us (80%)
  matrix products  25.2 us (7%)
  starting transfers between devices  20 us (6%)
  between operations  14 us (4%)
  local copies, waits for them, and re-layouts  3.93 us (1%)
    all_gather x1, waiting for transfers between devices, shards(): lax.all_gather(coupling, 'row', axis=0, tiled=True)  104 us
    all_gather x1, waiting for transfers between devices, shards(): lax.all_gather(first.astype(jnp.bfloat16), 'col', axis=1, tiled=True)  84.8 us
    all_gather x1, waiting for transfers between devices, shards(): target_block = lax.all_gather(target_dist, 'row', axis=0, tiled=True)  50.3 us
    dot_general x1, matrix products, shards(): jnp.dot(source_dist, lax.all_gather(coupling, 'row', axis=0, tiled=True),...  17.9 us
    all_to_all x2, waiting for transfers between devices, from_everyone(): return lax.all_to_all(copies, axis, split_axis=0, concat_axis=0, tiled=True)  17 us
    all_to_all x2, waiting for transfers between devices, summed_on_arrival(): lax.all_to_all(split_up(value, dim, length), axis, 0, 0, tiled=True)  14.2 us
    all_to_all x2, starting transfers between devices, from_everyone(): return lax.all_to_all(copies, axis, split_axis=0, concat_axis=0, tiled=True)  13.2 us
  transfers between devices with their start and end apart: 7, of which 7 were waited for; matrix products, arithmetic and copies ran while one was open for 6% of the time, Pallas kernels for 0%

commit v1 on v0

--- a/solution.py
+++ b/solution.py
@@ -106,7 +106,11 @@
         lax.all_gather(coupling, "row", axis=0, tiled=True),
         preferred_element_type=jnp.float32,
     )
-    first_whole = lax.all_gather(first.astype(jnp.bfloat16), "col", axis=1, tiled=True)
+    x = first.astype(jnp.bfloat16)
+    devices = lax.axis_size("col")
+    parts = jnp.stack([x for _ in range(devices)])
+    parts = lax.all_to_all(parts, "col", split_axis=0, concat_axis=0)
+    first_whole = jnp.concatenate(parts, axis=1)
     second = jnp.dot(first_whole, target_block, preferred_element_type=jnp.float32)
     affinity = lax.dot_general(
         source_feat, target_feat, (((1,), (1,)), ((), ())), preferred_element_type=jnp.float32

time: 337 us -> 284 us (0.84)
  waiting for transfers between devices: 271 us -> 211 us
  starting transfers between devices: 20 us -> 25.1 us
    all_gather x1 -> x0, waiting for transfers between devices: 84.8 us -> none  [shards(): lax.all_gather(first.astype(jnp.bfloat16), 'col', axis=1, tiled=True)]
    all_gather x1, waiting for transfers between devices: 50.3 us -> 75 us  [shards(): target_block = lax.all_gather(target_dist, 'row', axis=0, tiled=True)]
    all_to_all x0 -> x1, starting transfers between devices: none -> 5.94 us  [shards(): parts = lax.all_to_all(parts, 'col', split_axis=0, concat_axis=0)]
  transfers between devices with their start and end apart: 7 -> 7, of which waited for: 7 -> 6; matrix products, arithmetic and copies ran while one was open for 6% -> 8% of each run, Pallas kernels for 0% -> 0%
where the time goes in v1:
time: 284 us
  waiting for transfers between devices  211 us (74%)
  starting transfers between devices  25.1 us (9%)
  matrix products  24.5 us (9%)
  between operations  14.3 us (5%)
  local copies, waits for them, and re-layouts  6.48 us (2%)
    all_gather x1, waiting for transfers between devices, shards(): lax.all_gather(coupling, 'row', axis=0, tiled=True)  104 us
    all_gather x1, waiting for transfers between devices, shards(): target_block = lax.all_gather(target_dist, 'row', axis=0, tiled=True)  75 us
    dot_general x1, matrix products, shards(): jnp.dot(source_dist, lax.all_gather(coupling, 'row', axis=0, tiled=True),...  17.2 us
    all_to_all x2, waiting for transfers between devices, from_everyone(): return lax.all_to_all(copies, axis, split_axis=0, concat_axis=0, tiled=True)  17 us
    all_to_all x2, waiting for transfers between devices, summed_on_arrival(): lax.all_to_all(split_up(value, dim, length), axis, 0, 0, tiled=True)  14.2 us
    all_to_all x2, starting transfers between devices, from_everyone(): return lax.all_to_all(copies, axis, split_axis=0, concat_axis=0, tiled=True)  12.3 us
    all_to_all x2, starting transfers between devices, summed_on_arrival(): lax.all_to_all(split_up(value, dim, length), axis, 0, 0, tiled=True)  6.72 us
    all_to_all x1, starting transfers between devices, shards(): parts = lax.all_to_all(parts, 'col', split_axis=0, concat_axis=0)  5.94 us
  transfers between devices with their start and end apart: 7, of which 6 were waited for; matrix products, arithmetic and copies ran while one was open for 8% of the time, Pallas kernels for 0%

profile of v1, /device:TPU:8, one launch (start us, length us, event | category | flops | bytes accessed | tf_op | source)
XLA Modules:
  0.0 283.7 jit_solution(8209539310525563156)
XLA Ops:
  7.2 0.0 copy-start
  7.2 0.0 all-gather.3.cloned.1.call-start
  7.2 0.7 all-gather.3.cloned.1.call-update
  7.9 0.0 all-gather.5.cloned.1.call-start
  8.0 0.7 all-gather.5.cloned.1.call-update
  8.7 103.7 %all-gather.3.cloned.1.call-done = bf16[16384,512]{1,0:T(8,128)(2,1)} async-done(((bf16[512,512]{1,0:T(8,128)(2,1)}), bf16[16384,512]{1,0:T(8,128)(2,1)}) %all-gather.3.cloned.1.call-update) | async-done | bytes 16777232 | tf_op jit(solution)/shard_map/all_gather | solution.py:106
  112.4 17.2 %convolution_convert_fusion = bf16[512,512]{1,0:T(8,128)(2,1)S(1)} fusion(bf16[512,16384]{1,0:T(8,128)(2,1)} %param.10, bf16[16384,512]{1,0:T(8,128)(2,1)} %all-gather.3.cloned.1.call-done), kind=kOutput, calls=%fused_computation.5 | convolution fusion | flops 8590196736 | bytes 34078720 | tf_op jit(solution)/shard_map/dot_general | solution.py:104
  129.5 0.2 copy.21
  129.8 2.3 stack.2
  132.1 0.0 copy-start.1
  132.1 5.9 %all-to-all-start = ((bf16[8,512,512]{1,2,0:T(8,128)(2,1)}), bf16[8,512,512]{1,2,0:T(8,128)(2,1)}, u32[]{:S(2)}, u32[]{:S(2)}) async-start(bf16[8,512,512]{1,2,0:T(8,128)(2,1)} %stack.2), calls=%async_computation | async-start | bytes 8388608 | tf_op jit(solution)/shard_map/all_to_all | solution.py:112
  138.0 0.0 copy-done.1
  138.0 0.2 copy.20
  138.3 75.0 %all-gather.5.cloned.1.call-done = bf16[4096,512]{1,0:T(8,128)(2,1)} async-done(((bf16[128,512]{1,0:T(8,128)(2,1)}), bf16[4096,512]{1,0:T(8,128)(2,1)}) %all-gather.5.cloned.1.call-update) | async-done | bytes 4194320 | tf_op jit(solution)/shard_map/all_gather | solution.py:103
  213.3 0.0 all-to-all-done
  213.3 0.0 copy-start.2
  213.3 0.0 copy-start.5
  213.3 0.0 copy-start.6
  213.3 0.0 copy-start.3
  213.3 5.9 %fusion.2 = f32[512,512]{0,1:T(8,128)S(1)} fusion(bf16[512,4096]{0,1:T(8,128)(2,1)} %bitcast.1, bf16[4096,512]{1,0:T(8,128)(2,1)} %all-gather.5.cloned.1.call-done, bf16[512,512]{0,1:T(8,128)(2,1)S(1)} %copy.20), kind=kOutput, calls=%fused_computation.4 | convolution fusion | flops 2148270080 | bytes 9961472 | tf_op jit(solution)/shard_map/dot_general | solution.py:114
  219.2 0.0 copy-done
  219.2 0.0 copy-done.2
  219.2 0.0 copy-done.5
  219.2 0.0 copy-done.6
  219.2 0.0 copy-start.4
  219.2 0.4 fusion.12
  219.6 0.2 exponential_reduce_fusion.1
  219.8 0.6 broadcast_in_dim.4
  220.5 5.9 %all-to-all-start.1 = ((f32[8,2,512]{2,1,0:T(2,128)}), f32[8,2,512]{2,1,0:T(2,128)S(1)}, u32[]{:S(2)}, u32[]{:S(2)}) async-start(f32[8,2,512]{2,1,0:T(2,128)} %broadcast_in_dim.4), calls=%async_computation.1 | async-start | bytes 65536 | tf_op jit(solution)/shard_map/all_to_all | solution.py:14
  226.4 0.0 copy-done.3
  226.4 7.7 %all-to-all-done.1 = f32[8,2,512]{2,1,0:T(2,128)S(1)} async-done(((f32[8,2,512]{2,1,0:T(2,128)}), f32[8,2,512]{2,1,0:T(2,128)S(1)}, u32[]{:S(2)}, u32[]{:S(2)}) %all-to-all-start.1) | async-done | bytes 32800 | tf_op jit(solution)/shard_map/all_to_all | solution.py:14
  234.5 0.2 fusion.5
  234.7 0.4 exponential_reduce_fusion
  235.1 0.7 broadcast_in_dim.5
  235.7 6.4 %all-to-all-start.2 = ((f32[32,2,512]{2,1,0:T(2,128)}), f32[32,2,512]{2,1,0:T(2,128)S(1)}, u32[]{:S(2)}, u32[]{:S(2)}) async-start(f32[32,2,512]{2,1,0:T(2,128)} %broadcast_in_dim.5), calls=%async_computation.2 | async-start | bytes 262144 | tf_op jit(solution)/shard_map/all_to_all | solution.py:14
  242.2 0.0 copy-done.4
  242.2 9.2 %all-to-all-done.2 = f32[32,2,512]{2,1,0:T(2,128)S(1)} async-done(((f32[32,2,512]{2,1,0:T(2,128)}), f32[32,2,512]{2,1,0:T(2,128)S(1)}, u32[]{:S(2)}, u32[]{:S(2)}) %all-to-all-start.2) | async-done | bytes 131104 | tf_op jit(solution)/shard_map/all_to_all | solution.py:14
  251.4 0.1 fusion.10
  252.0 0.4 fusion.3
  252.4 0.7 convert_element_type.49
  253.1 3.3 %all-to-all-start.4 = ((bf16[8,64,1]{1,2,0:T(2,128)(2,1)}), bf16[8,64,1]{1,2,0:T(2,128)(2,1)S(1)}, u32[]{:S(2)}, u32[]{:S(2)}) async-start(bf16[8,64,1]{1,2,0:T(2,128)(2,1)} %convert_element_type.49), calls=%async_computation.4 | async-start | bytes 8192 | tf_op jit(solution)/shard_map/all_to_all | solution.py:76
  256.4 1.0 convolution_convert_fusion.1
  257.4 6.5 %all-to-all-done.4 = bf16[8,64,1]{1,2,0:T(2,128)(2,1)S(1)} async-done(((bf16[8,64,1]{1,2,0:T(2,128)(2,1)}), bf16[8,64,1]{1,2,0:T(2,128)(2,1)S(1)}, u32[]{:S(2)}, u32[]{:S(2)}) %all-to-all-start.4) | async-done | bytes 1056 | tf_op jit(solution)/shard_map/all_to_all | solution.py:76
  263.9 3.4 %all-to-all-start.3 = ((bf16[8,64,256]{2,1,0:T(8,128)(2,1)}), bf16[8,64,256]{2,1,0:T(8,128)(2,1)S(1)}, u32[]{:S(2)}, u32[]{:S(2)}) async-start(bf16[8,64,256]{2,1,0:T(8,128)(2,1)} %bitcast.10), calls=%async_computation.3 | async-start | bytes 524288 | tf_op jit(solution)/shard_map/all_to_all | solution.py:76
  267.4 1.0 copy.25
  268.4 7.7 %all-to-all-done.3 = bf16[8,64,256]{2,1,0:T(8,128)(2,1)S(1)} async-done(((bf16[8,64,256]{2,1,0:T(8,128)(2,1)}), bf16[8,64,256]{2,1,0:T(8,128)(2,1)S(1)}, u32[]{:S(2)}, u32[]{:S(2)}) %all-to-all-start.3) | async-done | bytes 262176 | tf_op jit(solution)/shard_map/all_to_all | solution.py:76
  276.1 0.7 divide_convert_fusion
  (42 shorter events, 0.8 us)
Async XLA Ops:
  7.2 212.0 %copy-start = (bf16[512,256]{1,0:T(8,128)(2,1)S(1)}, bf16[512,256]{1,0:T(8,128)(2,1)}, u32[]{:S(2)}) copy-start(bf16[512,256]{1,0:T(8,128)(2,1)} %param.13) | copy-start | bytes 786436
  7.2 105.2 %all-gather.3.cloned.1.call-start = ((), (), s32[]{:S(2)}) async-start(), calls=%async_computation.5 | async-start | bytes 17301504 | tf_op jit(solution)/shard_map/all_gather | solution.py:106
  7.9 205.3 %all-gather.5.cloned.1.call-start = ((), (), s32[]{:S(2)}) async-start(), calls=%async_computation.6 | async-start | bytes 4325376 | tf_op jit(solution)/shard_map/all_gather | solution.py:103
  132.1 5.9 %copy-start.1 = (bf16[512,512]{1,0:T(8,128)(2,1)S(1)}, bf16[512,512]{1,0:T(8,128)(2,1)}, u32[]{:S(2)}) copy-start(bf16[512,512]{1,0:T(8,128)(2,1)} %param.9) | copy-start | bytes 1572868
  132.1 81.2 %all-to-all-start = ((bf16[8,512,512]{1,2,0:T(8,128)(2,1)}), bf16[8,512,512]{1,2,0:T(8,128)(2,1)}, u32[]{:S(2)}, u32[]{:S(2)}) async-start(bf16[8,512,512]{1,2,0:T(8,128)(2,1)} %stack.2), calls=%async_computation | async-start | bytes 8388608 | tf_op jit(solution)/shard_map/all_to_all | solution.py:112
  213.3 5.9 %copy-start.2 = (bf16[512,256]{1,0:T(8,128)(2,1)S(1)}, bf16[512,256]{1,0:T(8,128)(2,1)}, u32[]{:S(2)}) copy-start(bf16[512,256]{1,0:T(8,128)(2,1)} %param.12) | copy-start | bytes 786436
  213.3 5.9 %copy-start.5 = (s32[512]{0:T(512)S(1)}, s32[512]{0:T(512)}, u32[]{:S(2)}) copy-start(s32[512]{0:T(512)} %param.15) | copy-start | bytes 6148
  213.3 5.9 %copy-start.6 = (s32[512]{0:T(512)S(1)}, s32[512]{0:T(512)}, u32[]{:S(2)}) copy-start(s32[512]{0:T(512)} %param.14) | copy-start | bytes 6148
  213.3 13.1 %copy-start.3 = (f32[512]{0:T(512)S(1)}, f32[512]{0:T(512)}, u32[]{:S(2)}) copy-start(f32[512]{0:T(512)} %param.16) | copy-start | bytes 6148
  219.2 23.0 %copy-start.4 = (f32[512]{0:T(512)S(1)}, f32[512]{0:T(512)}, u32[]{:S(2)}) copy-start(f32[512]{0:T(512)} %param.17) | copy-start | bytes 6148
  220.5 13.7 %all-to-all-start.1 = ((f32[8,2,512]{2,1,0:T(2,128)}), f32[8,2,512]{2,1,0:T(2,128)S(1)}, u32[]{:S(2)}, u32[]{:S(2)}) async-start(f32[8,2,512]{2,1,0:T(2,128)} %broadcast_in_dim.4), calls=%async_computation.1 | async-start | bytes 65536 | tf_op jit(solution)/shard_map/all_to_all | solution.py:14
  235.7 15.7 %all-to-all-start.2 = ((f32[32,2,512]{2,1,0:T(2,128)}), f32[32,2,512]{2,1,0:T(2,128)S(1)}, u32[]{:S(2)}, u32[]{:S(2)}) async-start(f32[32,2,512]{2,1,0:T(2,128)} %broadcast_in_dim.5), calls=%async_computation.2 | async-start | bytes 262144 | tf_op jit(solution)/shard_map/all_to_all | solution.py:14
  253.1 10.9 %all-to-all-start.4 = ((bf16[8,64,1]{1,2,0:T(2,128)(2,1)}), bf16[8,64,1]{1,2,0:T(2,128)(2,1)S(1)}, u32[]{:S(2)}, u32[]{:S(2)}) async-start(bf16[8,64,1]{1,2,0:T(2,128)(2,1)} %convert_element_type.49), calls=%async_computation.4 | async-start | bytes 8192 | tf_op jit(solution)/shard_map/all_to_all | solution.py:76
  263.9 12.1 %all-to-all-start.3 = ((bf16[8,64,256]{2,1,0:T(8,128)(2,1)}), bf16[8,64,256]{2,1,0:T(8,128)(2,1)S(1)}, u32[]{:S(2)}, u32[]{:S(2)}) async-start(bf16[8,64,256]{2,1,0:T(8,128)(2,1)} %bitcast.10), calls=%async_computation.3 | async-start | bytes 524288 | tf_op jit(solution)/shard_map/all_to_all | solution.py:76
Sparse Core Ops, SparseCore 0:
  9.8 102.4 all-gather.2
  114.2 98.9 all-gather.4
